TPU v7x, 512 devices: a whole 4x4x16 slice. The times are simulated.
512 devices in a mesh: grp: 16 (over y, x), tok: 32 (over z, core).
Axes of the slice: x: 4, y: 4, z: 16, core: 2. Of those that a mesh axis runs over, the one named last changes fastest.
Arguments:
- hidden_in: bfloat16 [16, 4096, 1024], P('grp', 'tok'), may hold values from -6 to 6
- lengths: int32 [16, 3], P('grp'), may hold values from 1 to 3072, 4096 in all within a row
- prefix_cache: bfloat16 [16, 512, 512], P('grp', 'tok'), may hold values from -2600 to 2600
- routes: int32 [16, 4096, 8], P('grp', 'tok'), may hold values from 0 to 31, all different within a row; in each aligned block of 128 rows (0 to 127, 128 to 255, ..., all dimensions but the last counted through in order) at most 40 rows name the same one
- gates: float32 [16, 4096, 8], P('grp', 'tok'), may hold values from 0.05 to 0.4
- attn_gain: float32 [1024], replicated, may hold values from 0.1 to 1.9
- w_qkv: bfloat16 [1024, 1024], P('grp', 'tok'), may hold values from -0.75 to 0.75
- w_out: bfloat16 [512, 1024], P('grp', 'tok'), may hold values from -0.25 to 0.25
- moe_gain: float32 [1024], replicated, may hold values from 0.1 to 1.9
- expert_gate_up: bfloat16 [32, 1024, 1024], P('tok', 'grp'), may hold values from -0.1875 to 0.1875
- expert_down: bfloat16 [32, 512, 1024], P('tok', 'grp'), may hold values from -0.25 to 0.25
Outputs:
- hidden_out: bfloat16 [16, 4096, 1024], P('grp', 'tok')
- suffix_cache: bfloat16 [16, 4096, 512], P('grp', 'tok')
Inputs may be any that keep to these rules, and one draw needn't show every extreme that they name: Each group's 3 lengths sum to 4096; no request is longer than 3072 tokens, and some request of every draw has exactly 3072. `routes`: each token names 8 different experts. Among the 128 tokens of one device no expert is named more than 40 times, a bound that some block reaches.
All inputs are finite; a program needn't handle non-finite values.
Results may differ from a plain program's by a relative error of at most 0.02.
Values may be sent and summed in bfloat16 or wider, within the bound.
A program may use at most 128 MiB of HBM per device.

v0:
```python
import jax
import jax.numpy as jnp
from jax import lax
from jax.sharding import PartitionSpec as P

HEADS = 8
KV_HEADS = 4
HEAD_DIM = 64
FF = 512
EXPERTS = 32
TOP = 8
CAP = 40
epsilon = 1e-05
score_scale = 0.015625
rope_base = 10000.0
big_negative = -1e30


def rms_scale(values, gain):
    values = values.astype(jnp.float32)
    mean_square = jnp.mean(values * values, axis=-1, keepdims=True)
    return values * lax.rsqrt(mean_square + epsilon) * gain


def request_layout(group_lengths, token_index):
    ends = jnp.cumsum(group_lengths)
    starts = ends - group_lengths
    segment = jnp.sum((token_index[:, None] >= ends[None, :]).astype(jnp.int32), axis=1)
    match = segment[:, None] == jnp.arange(group_lengths.shape[0], dtype=jnp.int32)[None, :]
    offset = token_index - jnp.sum(jnp.where(match, starts[None, :], 0), axis=1)
    return (segment, offset)


def rotate(values, position):
    half_width = values.shape[-1] // 2
    frequency = rope_base ** (-jnp.arange(half_width, dtype=jnp.float32) * 2.0 / values.shape[-1])
    angle = position.astype(jnp.float32)[:, None] * frequency[None, :]
    cosine = jnp.cos(angle)[:, None, :]
    sine = jnp.sin(angle)[:, None, :]
    first = values[..., :half_width]
    second = values[..., half_width:]
    return jnp.concatenate(
        [first * cosine - second * sine, second * cosine + first * sine], axis=-1
    )


def gather_small(blocks):
    flat = jnp.concatenate([b.reshape(-1) for b in blocks])
    gathered = lax.all_gather(flat[None], "tok", axis=0, tiled=True)
    pieces, start = ([], 0)
    for b in blocks:
        size = b.size
        pieces.append(gathered[:, start : start + size].reshape((-1,) + b.shape[1:]))
        start += size
    return pieces


def gather_rows(by_columns):
    return lax.all_gather(by_columns[None], "grp", axis=0, tiled=True)


def attend(carry, grouped, keys_values, allowed):
    best, total, mixed = carry
    key_count = keys_values.shape[0]
    key_width = KV_HEADS * HEAD_DIM
    key_heads = keys_values[:, :key_width].reshape(key_count, KV_HEADS, HEAD_DIM).transpose(1, 0, 2)
    value_heads = (
        keys_values[:, key_width:].reshape(key_count, KV_HEADS, HEAD_DIM).transpose(1, 0, 2)
    )
    scores = (
        jnp.einsum("kqd,knd->kqn", grouped, key_heads, preferred_element_type=jnp.float32)
        * score_scale
    )
    if allowed is not None:
        row_count = grouped.shape[1]
        share = row_count // allowed.shape[0]
        mask = jnp.broadcast_to(allowed[:, None, :], (allowed.shape[0], share, key_count)).reshape(
            row_count, key_count
        )
        scores = jnp.where(mask[None], scores, big_negative)
    new_best = jnp.maximum(best, jnp.max(scores, axis=-1))
    factor = jnp.exp(best - new_best)
    probs = jnp.exp(scores - new_best[..., None])
    total = total * factor + jnp.sum(probs, axis=-1)
    mixed = mixed * factor[..., None] + jnp.einsum(
        "kqn,knd->kqd", probs.astype(jnp.bfloat16), value_heads, preferred_element_type=jnp.float32
    )
    return (new_best, total, mixed)


def local(
    hidden_in,
    lengths,
    prefix_cache,
    routes,
    gates,
    attn_gain,
    w_qkv,
    w_out,
    moe_gain,
    expert_gate_up,
    expert_down,
):
    tokens_here = hidden_in[0]
    tok_count = tokens_here.shape[0]
    axis_count = lax.axis_size("tok")
    device_place = lax.axis_index("tok")
    group_lengths = lengths[0]
    token_index = device_place * tok_count + jnp.arange(tok_count, dtype=jnp.int32)
    segment, offset = request_layout(group_lengths, token_index)
    position = prefix_cache.shape[1] * axis_count + offset
    query_width = HEADS * HEAD_DIM
    key_width = KV_HEADS * HEAD_DIM
    group_share = HEADS // KV_HEADS
    normed = rms_scale(tokens_here, attn_gain).astype(jnp.bfloat16)
    qkv_columns, out_columns, prefix_all = gather_small([w_qkv.T, w_out.T, prefix_cache[0]])
    qkv_weight = gather_rows(qkv_columns)
    projected = jnp.einsum(
        "ngr,gcr->nc",
        normed.reshape(tok_count, qkv_weight.shape[0], qkv_weight.shape[2]),
        qkv_weight,
        preferred_element_type=jnp.float32,
    )
    query = rotate(projected[:, :query_width].reshape(tok_count, HEADS, HEAD_DIM), position).astype(
        jnp.bfloat16
    )
    keys_new = rotate(
        projected[:, query_width : query_width + key_width].reshape(tok_count, KV_HEADS, HEAD_DIM),
        position,
    ).astype(jnp.bfloat16)
    values_new = projected[:, query_width + key_width :].astype(jnp.bfloat16)
    suffix_cache = jnp.concatenate([keys_new.reshape(tok_count, key_width), values_new], axis=1)
    row_count = tok_count * group_share
    grouped = (
        query.reshape(tok_count, KV_HEADS, group_share, HEAD_DIM)
        .transpose(1, 0, 2, 3)
        .reshape(KV_HEADS, row_count, HEAD_DIM)
    )
    start_carry = (
        jnp.full((KV_HEADS, row_count), big_negative, jnp.float32),
        jnp.zeros((KV_HEADS, row_count), jnp.float32),
        jnp.zeros((KV_HEADS, row_count, HEAD_DIM), jnp.float32),
    )
    carry = attend(start_carry, grouped, prefix_all, None)
    piece = lax.all_gather(suffix_cache, "tok", axis=0, tiled=True)
    key_index = jnp.arange(piece.shape[0], dtype=jnp.int32)
    key_segment, key_offset = request_layout(group_lengths, key_index)
    earlier = key_index[None, :] <= token_index[:, None]
    same_request = key_segment[None, :] == segment[:, None]
    carry = attend(carry, grouped, piece, earlier & same_request & (key_index[None, :] >= 0))
    best, total, mixed = carry
    attended = (mixed / total[..., None]).reshape(KV_HEADS, tok_count, group_share, HEAD_DIM)
    attended = attended.transpose(1, 0, 2, 3).reshape(tok_count, query_width).astype(jnp.bfloat16)
    out_weight = gather_rows(out_columns)
    projected_out = jnp.einsum(
        "ngr,gcr->nc",
        attended.reshape(tok_count, out_weight.shape[0], out_weight.shape[2]),
        out_weight,
        preferred_element_type=jnp.float32,
    )
    after_attention = tokens_here.astype(jnp.float32) + projected_out
    moe_in = rms_scale(after_attention, moe_gain).astype(jnp.bfloat16)
    model_width = moe_in.shape[1]
    flat_routes = routes[0].reshape(-1)
    onehot = (flat_routes[:, None] == jnp.arange(EXPERTS, dtype=jnp.int32)[None, :]).astype(
        jnp.int32
    )
    slot_rank = jnp.sum(jnp.cumsum(onehot, axis=0) * onehot, axis=1) - 1
    slot_index = flat_routes * CAP + slot_rank
    source_token = jnp.arange(flat_routes.shape[0], dtype=jnp.int32) // TOP
    outgoing = (
        jnp.zeros((EXPERTS * CAP, model_width), jnp.bfloat16)
        .at[slot_index]
        .set(moe_in[source_token])
    )
    arrived = lax.all_to_all(
        outgoing.reshape(EXPERTS, CAP, model_width), "tok", split_axis=0, concat_axis=0, tiled=True
    ).reshape(1, EXPERTS * CAP, model_width)
    sliced = arrived
    hidden_pair = jnp.einsum(
        "erd,edf->erf",
        sliced,
        lax.all_gather(expert_gate_up, "grp", axis=1, tiled=True),
        preferred_element_type=jnp.float32,
    )
    activated = (jax.nn.silu(hidden_pair[..., :FF]) * hidden_pair[..., FF:]).astype(jnp.bfloat16)
    sliced = activated
    expert_result = jnp.einsum(
        "erf,efd->erd",
        sliced,
        lax.all_gather(expert_down, "grp", axis=1, tiled=True),
        preferred_element_type=jnp.float32,
    ).astype(jnp.bfloat16)
    returned = lax.all_to_all(
        expert_result.reshape(EXPERTS, CAP, model_width),
        "tok",
        split_axis=0,
        concat_axis=0,
        tiled=True,
    ).reshape(EXPERTS * CAP, -1)
    weighted = returned[slot_index].astype(jnp.float32) * gates[0].reshape(-1)[:, None]
    moe_out = jnp.sum(weighted.reshape(tok_count, TOP, -1), axis=1)
    hidden_out = (after_attention + moe_out).astype(jnp.bfloat16)
    return (hidden_out[None], suffix_cache[None])


def solution(mesh):
    return jax.shard_map(
        local,
        mesh=mesh,
        in_specs=(
            P("grp", "tok", None),
            P("grp", None),
            P("grp", "tok", None),
            P("grp", "tok", None),
            P("grp", "tok", None),
            P(),
            P("grp", "tok"),
            P("grp", "tok"),
            P(),
            P("tok", "grp", None),
            P("tok", "grp", None),
        ),
        out_specs=(P("grp", "tok", None), P("grp", "tok", None)),
        check_vma=False,
    )
```

profile of v0, /device:TPU:32, one launch (start us, length us, event | category | flops | bytes accessed | tf_op | source)
XLA Modules:
  0.0 550.5 jit_solution(17672893901105111063)
XLA Ops:
  7.2 0.8 copy.113
  8.0 0.8 copy.89
  8.9 0.8 reshape.360
  9.7 36.1 %all-gather = bf16[360448]{0:T(1024)(128)(2,1)S(1)} all-gather(bf16[11264]{0:T(1024)(128)(2,1)S(1)} %pad_maximum_fusion.3), channel_id=2, replica_groups=mesh['grp'=16,'tok'=32] {'tok'}, dimensions={0}, use_global_device_ids=true | all-gather | bytes 743424 | tf_op jit(solution)/shard_map/all_gather | solution.py:49
  45.7 0.3 reshape.407
  46.0 0.2 broadcast_in_dim_reshape.7
  46.3 0.8 copy.90
  47.2 0.1 copy.88
  47.4 0.2 reduce-window.10
  47.8 0.1 fusion.26
  47.9 0.1 multiply_cosine_fusion
  48.1 57.2 %all-gather.7.cloned.1.call-done = bf16[16,1024,64]{1,2,0:T(8,128)(2,1)} async-done(((bf16[1,1024,64]{1,2,0:T(8,128)(2,1)}), bf16[16,1024,64]{1,2,0:T(8,128)(2,1)}) %all-gather.7.cloned.1.call-update) | async-done | bytes 2097168 | tf_op jit(solution)/shard_map/all_gather | solution.py:59
  105.3 2.3 convolution_bitcast_fusion.2
  107.6 0.8 copy-done.4
  108.6 0.1 copy.98
  108.7 0.7 fusion.39
  109.4 0.2 all-gather.11.cloned.1.call-start
  109.7 0.2 broadcast_in_dim_reshape.8
  109.8 0.7 copy.104
  110.6 0.1 convert_reduce_fusion
  110.7 0.9 slice.81
  111.9 0.5 fusion.11
  112.4 2.4 broadcast_in_dim.44
  114.8 2.6 broadcast_in_dim.49
  117.4 1.3 reshape.366
  118.8 0.1 copy.94
  118.9 0.9 copy.96
  120.0 9.0 %reduce-window.11 = s32[32,8,128]{2,1,0:T(8,128)S(1)} reduce-window(s32[32,8,128]{2,1,0:T(8,128)S(1)} %fusion.32, s32[]{:T(128)} %constant.34.clone.1), window={size=1x1x128 pad=0_0x0_0x127_0}, to_apply=%region_9.10 | reduce-window | flops 4161536 | bytes 262148 | tf_op jit(solution)/shard_map/reduce-window.1
  129.1 0.1 copy.108
  129.3 0.1 broadcast_add_fusion
  129.6 0.1 copy.91
  129.7 0.2 copy.93
  129.9 0.2 copy.92
  130.1 0.7 pad_maximum_fusion
  130.8 1.8 multiply_reduce_fusion
  132.6 50.5 %all-gather.9.cloned.1.call-done = bf16[4096,512]{1,0:T(8,128)(2,1)} async-done(((bf16[128,512]{1,0:T(8,128)(2,1)}), bf16[4096,512]{1,0:T(8,128)(2,1)}) %all-gather.9.cloned.1.call-update) | async-done | bytes 4194320 | tf_op jit(solution)/shard_map/all_gather | solution.py:145
  183.1 3.8 fusion.40
  186.9 2.9 copy.101
  189.8 2.9 copy.99
  192.8 3.5 fusion
  196.3 4.6 fusion.1
  200.9 1.7 copy-done
  202.6 0.5 fusion.12
  203.2 11.2 %fusion.3 = f32[4,256,64]{1,2,0:T(8,128)} fusion(bf16[4,4096,64]{1,2,0:T(8,128)(2,1)} %bitcast.104, f32[4,256,4096]{2,1,0:T(8,128)} %copy-done, f32[4,256]{1,0:T(4,128)S(1)} %get-tuple-element.15, pred[256,4096]{1,0:T(8,128)(4,1)S(1)} %broadcast_in_dim.49), kind=kOutput, calls=%fused_computation.8 | convolution fusion | flops 553648128 | bytes 20189184 | tf_op jit(solution)/shard_map/kqn,knd->kqd/dot_general | solution.py:85
  214.5 1.6 fusion.21
  216.1 0.2 copy.102
  216.2 0.1 copy.103
  216.4 24.7 %all-gather.11.cloned.1.call-done = bf16[16,1024,32]{1,2,0:T(8,128)(2,1)} async-done(((bf16[1,1024,32]{1,2,0:T(8,128)(2,1)}), bf16[16,1024,32]{1,2,0:T(8,128)(2,1)}) %all-gather.11.cloned.1.call-update) | async-done | bytes 1048592 | tf_op jit(solution)/shard_map/all_gather | solution.py:59
  241.1 1.6 multiply_reduce_fusion.1
  242.7 0.1 multiply_convert_fusion
  242.8 14.7 %scatter_custom_fusion = bf16[1280,1024]{1,0:T(8,128)(2,1)} fusion(s32[1024]{0:T(1024)S(1)} %bitcast.118, bf16[128,1024]{1,0:T(8,128)(2,1)S(1)} %multiply_convert_fusion, s32[1024]{0:T(1024)S(1)} %broadcast_clamp_fusion.1, bf16[]{:T(256)} %constant.67.clone.1), kind=kCustom, calls=%fused_computation.17 | custom fusion | bytes 2621442 | tf_op jit(solution)/shard_map/scatter | solution.py:174
  257.6 12.8 %all-to-all-start = ((bf16[32,40,1024]{2,1,0:T(8,128)(2,1)}), bf16[32,40,1024]{2,1,0:T(8,128)(2,1)S(1)}, u32[]{:S(2)}, u32[]{:S(2)}) async-start(bf16[32,40,1024]{2,1,0:T(8,128)(2,1)} %bitcast.34), calls=%async_computation | async-start | bytes 5242880 | tf_op jit(solution)/shard_map/all_to_all | solution.py:176
  270.5 0.5 all-gather.13.cloned.1.call-update
  271.0 0.5 all-gather.15.cloned.1.call-update
  271.6 61.4 %all-gather.13.cloned.1.call-done = bf16[1,1024,1024]{2,1,0:T(8,128)(2,1)} async-done(((bf16[1,64,1024]{2,1,0:T(8,128)(2,1)}), bf16[1,1024,1024]{2,1,0:T(8,128)(2,1)}) %all-gather.13.cloned.1.call-update) | async-done | bytes 2097168 | tf_op jit(solution)/shard_map/all_gather | solution.py:183
  332.9 60.2 %all-to-all-done = bf16[32,40,1024]{2,1,0:T(8,128)(2,1)S(1)} async-done(((bf16[32,40,1024]{2,1,0:T(8,128)(2,1)}), bf16[32,40,1024]{2,1,0:T(8,128)(2,1)S(1)}, u32[]{:S(2)}, u32[]{:S(2)}) %all-to-all-start) | async-done | bytes 2621472 | tf_op jit(solution)/shard_map/all_to_all | solution.py:176
  393.1 6.2 %convolution_bitcast_fusion = f32[1,1280,1024]{2,1,0:T(8,128)} fusion(bf16[1280,1024]{1,0:T(8,128)(2,1)S(1)} %bitcast.102, bf16[1,1024,1024]{2,1,0:T(8,128)(2,1)} %all-gather.13.cloned.1.call-done), kind=kOutput, calls=%fused_computation.10 | convolution fusion | flops 2684354560 | bytes 9961472 | tf_op jit(solution)/shard_map/erd,edf->erf/dot_general | solution.py:180
  399.3 5.9 %convolution_convert_fusion = bf16[1280,1024]{1,0:T(8,128)(2,1)} fusion(f32[1,1280,1024]{2,1,0:T(8,128)} %convolution_bitcast_fusion, bf16[1,512,1024]{2,1,0:T(8,128)(2,1)} %all-gather.15.cloned.1.call-done), kind=kOutput, calls=%fused_computation.13 | convolution fusion | flops 1347420160 | bytes 8912896 | tf_op jit(solution)/shard_map/erf,efd->erd/dot_general | solution.py:188
  405.2 6.9 %all-to-all-start.1 = ((bf16[32,40,1024]{2,1,0:T(8,128)(2,1)}), bf16[32,40,1024]{2,1,0:T(8,128)(2,1)S(1)}, u32[]{:S(2)}, u32[]{:S(2)}) async-start(bf16[32,40,1024]{2,1,0:T(8,128)(2,1)} %bitcast.103), calls=%async_computation.1 | async-start | bytes 5242880 | tf_op jit(solution)/shard_map/all_to_all | solution.py:194
  412.2 0.1 copy.110
  412.3 122.6 %all-to-all-done.1 = bf16[32,40,1024]{2,1,0:T(8,128)(2,1)S(1)} async-done(((bf16[32,40,1024]{2,1,0:T(8,128)(2,1)}), bf16[32,40,1024]{2,1,0:T(8,128)(2,1)S(1)}, u32[]{:S(2)}, u32[]{:S(2)}) %all-to-all-start.1) | async-done | bytes 2621472 | tf_op jit(solution)/shard_map/all_to_all | solution.py:194
  534.9 5.4 gather_fusion
  540.2 2.9 fusion.6
  543.2 0.8 fusion.27
  (69 shorter events, 1.7 us)
Async XLA Ops:
  7.2 40.0 %copy-start.2 = (bf16[1,128,1024]{2,1,0:T(8,128)(2,1)S(1)}, bf16[1,128,1024]{2,1,0:T(8,128)(2,1)}, u32[]{:S(2)}) copy-start(bf16[1,128,1024]{2,1,0:T(8,128)(2,1)} %param.11) | copy-start | bytes 786436
  7.2 40.1 %copy-start.8 = (f32[1024]{0:T(1024)S(1)}, f32[1024]{0:T(1024)}, u32[]{:S(2)}) copy-start(f32[1024]{0:T(1024)} %param.16) | copy-start | bytes 12292
  7.2 40.2 %copy-start.10 = (s32[1,3]{1,0:T(1,128)S(1)}, s32[1,3]{1,0:T(1,128)}, u32[]{:S(2)}) copy-start(s32[1,3]{1,0:T(1,128)} %param.12) | copy-start | bytes 40
  7.2 98.1 %all-gather.7.cloned.1.call-start = ((), (), s32[]{:S(2)}) async-start(), calls=%async_computation.2 | async-start | bytes 2228224 | tf_op jit(solution)/shard_map/all_gather | solution.py:59
  47.1 136.0 %all-gather.9.cloned.1.call-start = ((), (), s32[]{:S(2)}) async-start(), calls=%async_computation.3 | async-start | bytes 4325376 | tf_op jit(solution)/shard_map/all_gather | solution.py:145
  105.3 6.3 %copy-start.6 = (s32[1,128,8]{1,2,0:T(8,128)S(1)}, s32[1,128,8]{1,2,0:T(8,128)}, u32[]{:S(2)}) copy-start(s32[1,128,8]{1,2,0:T(8,128)} %param.14) | copy-start | bytes 12292
  107.6 0.8 copy-start.4
  109.4 131.6 %all-gather.11.cloned.1.call-start = ((), (), s32[]{:S(2)}) async-start(), calls=%async_computation.4 | async-start | bytes 1114112 | tf_op jit(solution)/shard_map/all_gather | solution.py:59
  117.4 12.2 %slice-start = ((f32[128,1024]{1,0:T(8,128)}), f32[128,512]{1,0:T(8,128)S(1)}, s32[]{:S(2)}) async-start(f32[128,1024]{1,0:T(8,128)} %copy-done.4), calls=%async_computation.7 | async-start | bytes 524288 | tf_op jit(solution)/shard_map/slice | solution.py:124
  196.2 6.4 %copy-start = (f32[4,256,4096]{2,1,0:T(8,128)}, f32[4,256,4096]{2,1,0:T(8,128)S(1)}, u32[]{:S(2)}) copy-start(f32[4,256,4096]{2,1,0:T(8,128)S(1)} %get-tuple-element.22) | copy-start | bytes 50331652
  196.3 6.4 %copy-start.1 = (f32[4,256,512]{2,1,0:T(8,128)S(1)}, f32[4,256,512]{2,1,0:T(8,128)}, u32[]{:S(2)}) copy-start(f32[4,256,512]{2,1,0:T(8,128)} %get-tuple-element.20) | copy-start | bytes 6291460
  203.2 11.2 %copy-start.5 = (bf16[512,256]{0,1:T(8,128)(2,1)S(1)}, bf16[512,256]{0,1:T(8,128)(2,1)}, u32[]{:S(2)}) copy-start(bf16[512,256]{0,1:T(8,128)(2,1)} %copy.96) | copy-start | bytes 786436
  214.5 26.6 %copy-start.3 = (bf16[1,128,1024]{2,1,0:T(8,128)(2,1)S(1)}, bf16[1,128,1024]{2,1,0:T(8,128)(2,1)}, u32[]{:S(2)}) copy-start(bf16[1,128,1024]{2,1,0:T(8,128)(2,1)} %param.11) | copy-start | bytes 786436
  214.5 28.3 %copy-start.7 = (f32[1024]{0:T(1024)S(1)}, f32[1024]{0:T(1024)}, u32[]{:S(2)}) copy-start(f32[1024]{0:T(1024)} %param.19) | copy-start | bytes 12292
  257.6 135.5 %all-to-all-start = ((bf16[32,40,1024]{2,1,0:T(8,128)(2,1)}), bf16[32,40,1024]{2,1,0:T(8,128)(2,1)S(1)}, u32[]{:S(2)}, u32[]{:S(2)}) async-start(bf16[32,40,1024]{2,1,0:T(8,128)(2,1)} %bitcast.34), calls=%async_computation | async-start | bytes 5242880 | tf_op jit(solution)/shard_map/all_to_all | solution.py:176
  270.4 62.5 %all-gather.13.cloned.1.call-start = ((), (), s32[]{:S(2)}) async-start(), calls=%async_computation.5 | async-start | bytes 2228224 | tf_op jit(solution)/shard_map/all_gather | solution.py:183
  271.0 128.3 %all-gather.15.cloned.1.call-start = ((), (), s32[]{:S(2)}) async-start(), calls=%async_computation.6 | async-start | bytes 1114112 | tf_op jit(solution)/shard_map/all_gather | solution.py:191
  405.2 6.9 %copy-start.9 = (f32[1,128,8]{1,2,0:T(8,128)S(1)}, f32[1,128,8]{1,2,0:T(8,128)}, u32[]{:S(2)}) copy-start(f32[1,128,8]{1,2,0:T(8,128)} %param.15) | copy-start | bytes 12292
  405.2 129.7 %all-to-all-start.1 = ((bf16[32,40,1024]{2,1,0:T(8,128)(2,1)}), bf16[32,40,1024]{2,1,0:T(8,128)(2,1)S(1)}, u32[]{:S(2)}, u32[]{:S(2)}) async-start(bf16[32,40,1024]{2,1,0:T(8,128)(2,1)} %bitcast.103), calls=%async_computation.1 | async-start | bytes 5242880 | tf_op jit(solution)/shard_map/all_to_all | solution.py:194
Sparse Core Ops, SparseCore 0:
  47.2 58.0 all-gather.6
  109.5 73.5 all-gather.8
  186.1 54.9 all-gather.10
  273.9 58.9 all-gather.12
  335.8 57.4 all-gather.14
where the time goes:
time: 551 us; the launch traced here: 550 us
  waiting for transfers between devices  378 us (69%)
  local copies, waits for them, and re-layouts  47.2 us (9%)
  blocking collectives  36.1 us (7%)
  matrix products  34.1 us (6%)
  other arithmetic  21 us (4%)
  starting transfers between devices  20.1 us (4%)
  between operations  14.3 us (3%)
    all_to_all x1, waiting for transfers between devices, local(): lax.all_to_all(expert_result.reshape(EXPERTS, CAP, model_width), 'tok', s...  123 us
    all_gather x2, waiting for transfers between devices, gather_rows(): return lax.all_gather(by_columns[None], 'grp', axis=0, tiled=True)  81.9 us
    all_gather x1, waiting for transfers between devices, local(): lax.all_gather(expert_gate_up, 'grp', axis=1, tiled=True)  61.4 us
    all_to_all x1, waiting for transfers between devices, local(): lax.all_to_all(outgoing.reshape(EXPERTS, CAP, model_width), 'tok', split_...  60.2 us
    all_gather x1, waiting for transfers between devices, local(): piece = lax.all_gather(suffix_cache, 'tok', axis=0, tiled=True)  50.5 us
    all_gather x1, blocking collectives, gather_small(): gathered = lax.all_gather(flat[None], 'tok', axis=0, tiled=True)  36.1 us
    scatter x1, local copies, waits for them, and re-layouts, local(): outgoing = jnp.zeros((EXPERTS * CAP, model_width), jnp.bfloat16).at[slot_...  14.7 us
    dot_general x2, matrix products, attend(): jnp.einsum('kqn,knd->kqd', probs.astype(jnp.bfloat16), value_heads, prefe...  12.8 us
  transfers between devices with their start and end apart: 7, of which 6 were waited for; matrix products, arithmetic and copies ran while one was open for 11% of the time, Pallas kernels for 0%

commit v1 on v0

--- a/solution.py
+++ b/solution.py
@@ -180,7 +180,9 @@
     hidden_pair = jnp.einsum(
         "erd,edf->erf",
         sliced,
-        lax.all_gather(expert_gate_up, "grp", axis=1, tiled=True),
+        jnp.concatenate(
+            lax.all_to_all(jnp.stack([expert_gate_up] * lax.axis_size("grp")), "grp", 0, 0), axis=1
+        ),
         preferred_element_type=jnp.float32,
     )
     activated = (jax.nn.silu(hidden_pair[..., :FF]) * hidden_pair[..., FF:]).astype(jnp.bfloat16)

time: 551 us -> 548 us (level)
  waiting for transfers between devices: 378 us -> 371 us
    all_to_all x1, waiting for transfers between devices: 60.2 us -> 122 us  [local(): lax.all_to_all(outgoing.reshape(EXPERTS, CAP, model_width), 'tok', split_...]
    all_gather x1 -> x0, waiting for transfers between devices: 61.4 us -> none  [local(): lax.all_gather(expert_gate_up, 'grp', axis=1, tiled=True)]
    all_gather x1, waiting for transfers between devices: 50.5 us -> 43.7 us  [local(): piece = lax.all_gather(suffix_cache, 'tok', axis=0, tiled=True)]
  transfers between devices with their start and end apart: 7 -> 7, of which waited for: 6 -> 5; matrix products, arithmetic and copies ran while one was open for 11% -> 15% of each run, Pallas kernels for 0% -> 0%
where the time goes in v1:
time: 548 us; the launch traced here: 547 us
  waiting for transfers between devices  371 us (68%)
  local copies, waits for them, and re-layouts  48.9 us (9%)
  blocking collectives  36.1 us (7%)
  matrix products  34.1 us (6%)
  starting transfers between devices  22.3 us (4%)
  other arithmetic  21 us (4%)
  between operations  14.2 us (3%)
    all_to_all x1, waiting for transfers between devices, local(): lax.all_to_all(expert_result.reshape(EXPERTS, CAP, model_width), 'tok', s...  122 us
    all_to_all x1, waiting for transfers between devices, local(): lax.all_to_all(outgoing.reshape(EXPERTS, CAP, model_width), 'tok', split_...  122 us
    all_gather x2, waiting for transfers between devices, gather_rows(): return lax.all_gather(by_columns[None], 'grp', axis=0, tiled=True)  82 us
    all_gather x1, waiting for transfers between devices, local(): piece = lax.all_gather(suffix_cache, 'tok', axis=0, tiled=True)  43.7 us
    all_gather x1, blocking collectives, gather_small(): gathered = lax.all_gather(flat[None], 'tok', axis=0, tiled=True)  36.1 us
    scatter x1, local copies, waits for them, and re-layouts, local(): outgoing = jnp.zeros((EXPERTS * CAP, model_width), jnp.bfloat16).at[slot_...  14.7 us
    dot_general x2, matrix products, attend(): jnp.einsum('kqn,knd->kqd', probs.astype(jnp.bfloat16), value_heads, prefe...  12.8 us
    all_to_all x1, starting transfers between devices, local(): lax.all_to_all(outgoing.reshape(EXPERTS, CAP, model_width), 'tok', split_...  12.8 us
  transfers between devices with their start and end apart: 7, of which 5 were waited for; matrix products, arithmetic and copies ran while one was open for 15% of the time, Pallas kernels for 0%

profile of v1, /device:TPU:32, one launch (start us, length us, event | category | flops | bytes accessed | tf_op | source)
XLA Modules:
  0.0 547.2 jit_solution(11317888462294164468)
XLA Ops:
  7.2 0.8 copy.113
  8.0 0.8 copy.89
  8.9 0.8 reshape.365
  9.7 36.1 %all-gather = bf16[360448]{0:T(1024)(128)(2,1)S(1)} all-gather(bf16[11264]{0:T(1024)(128)(2,1)S(1)} %pad_maximum_fusion.3), channel_id=2, replica_groups=mesh['grp'=16,'tok'=32] {'tok'}, dimensions={0}, use_global_device_ids=true | all-gather | bytes 743424 | tf_op jit(solution)/shard_map/all_gather | solution.py:49
  45.7 0.3 reshape.412
  46.0 0.2 broadcast_in_dim_reshape.7
  46.3 0.8 copy.90
  47.2 0.1 copy.88
  47.4 0.2 reduce-window.10
  47.8 0.1 fusion.25
  47.9 0.1 multiply_cosine_fusion
  48.1 57.2 %all-gather.6.cloned.1.call-done = bf16[16,1024,64]{1,2,0:T(8,128)(2,1)} async-done(((bf16[1,1024,64]{1,2,0:T(8,128)(2,1)}), bf16[16,1024,64]{1,2,0:T(8,128)(2,1)}) %all-gather.6.cloned.1.call-update) | async-done | bytes 2097168 | tf_op jit(solution)/shard_map/all_gather | solution.py:59
  105.3 2.3 convolution_bitcast_fusion.2
  107.6 0.8 copy-done.4
  108.5 0.1 copy.98
  108.7 0.7 fusion.38
  109.4 1.6 stack.2
  111.0 5.1 all-to-all-start.1
  116.1 0.2 all-gather.10.cloned.1.call-start
  116.3 0.2 broadcast_in_dim_reshape.8
  116.5 0.7 copy.104
  117.3 0.1 convert_reduce_fusion
  117.4 0.9 slice.81
  118.6 0.5 fusion.10
  119.1 2.4 broadcast_in_dim.44
  121.5 2.6 broadcast_in_dim.49
  124.1 1.3 reshape.371
  125.5 0.1 copy.94
  125.6 0.9 copy.96
  126.7 9.0 %reduce-window.11 = s32[32,8,128]{2,1,0:T(8,128)S(1)} reduce-window(s32[32,8,128]{2,1,0:T(8,128)S(1)} %fusion.31, s32[]{:T(128)} %constant.34.clone.1), window={size=1x1x128 pad=0_0x0_0x127_0}, to_apply=%region_9.10 | reduce-window | flops 4161536 | bytes 262148 | tf_op jit(solution)/shard_map/reduce-window.1
  135.8 0.1 copy.108
  136.0 0.1 broadcast_add_fusion
  136.2 0.1 copy.91
  136.4 0.2 copy.93
  136.6 0.2 copy.92
  136.8 0.7 pad_maximum_fusion
  137.5 1.7 multiply_reduce_fusion
  139.2 43.7 %all-gather.8.cloned.1.call-done = bf16[4096,512]{1,0:T(8,128)(2,1)} async-done(((bf16[128,512]{1,0:T(8,128)(2,1)}), bf16[4096,512]{1,0:T(8,128)(2,1)}) %all-gather.8.cloned.1.call-update) | async-done | bytes 4194320 | tf_op jit(solution)/shard_map/all_gather | solution.py:145
  182.9 3.8 fusion.39
  186.8 3.0 copy.101
  189.8 2.9 copy.99
  192.7 3.5 fusion
  196.2 4.6 fusion.1
  200.9 1.7 copy-done
  202.6 0.5 fusion.11
  203.2 11.2 %fusion.3 = f32[4,256,64]{1,2,0:T(8,128)} fusion(bf16[4,4096,64]{1,2,0:T(8,128)(2,1)} %bitcast.104, f32[4,256,4096]{2,1,0:T(8,128)} %copy-done, f32[4,256]{1,0:T(4,128)S(1)} %get-tuple-element.15, pred[256,4096]{1,0:T(8,128)(4,1)S(1)} %broadcast_in_dim.49), kind=kOutput, calls=%fused_computation.8 | convolution fusion | flops 553648128 | bytes 20189184 | tf_op jit(solution)/shard_map/kqn,knd->kqd/dot_general | solution.py:85
  214.4 1.6 fusion.20
  216.0 0.2 copy.102
  216.2 0.1 copy.103
  216.3 24.8 %all-gather.10.cloned.1.call-done = bf16[16,1024,32]{1,2,0:T(8,128)(2,1)} async-done(((bf16[1,1024,32]{1,2,0:T(8,128)(2,1)}), bf16[16,1024,32]{1,2,0:T(8,128)(2,1)}) %all-gather.10.cloned.1.call-update) | async-done | bytes 1048592 | tf_op jit(solution)/shard_map/all_gather | solution.py:59
  241.1 1.6 multiply_reduce_fusion.1
  242.8 0.1 multiply_convert_fusion
  242.9 14.7 %scatter_custom_fusion = bf16[1280,1024]{1,0:T(8,128)(2,1)} fusion(s32[1024]{0:T(1024)S(1)} %bitcast.119, bf16[128,1024]{1,0:T(8,128)(2,1)S(1)} %multiply_convert_fusion, s32[1024]{0:T(1024)S(1)} %broadcast_clamp_fusion.1, bf16[]{:T(256)} %constant.67.clone.1), kind=kCustom, calls=%fused_computation.16 | custom fusion | bytes 2621442 | tf_op jit(solution)/shard_map/scatter | solution.py:174
  257.7 12.8 %all-to-all-start = ((bf16[32,40,1024]{2,1,0:T(8,128)(2,1)}), bf16[32,40,1024]{2,1,0:T(8,128)(2,1)S(1)}, u32[]{:S(2)}, u32[]{:S(2)}) async-start(bf16[32,40,1024]{2,1,0:T(8,128)(2,1)} %bitcast.34), calls=%async_computation | async-start | bytes 5242880 | tf_op jit(solution)/shard_map/all_to_all | solution.py:176
  270.5 0.5 all-gather.12.cloned.1.call-update
  271.1 122.2 %all-to-all-done = bf16[32,40,1024]{2,1,0:T(8,128)(2,1)S(1)} async-done(((bf16[32,40,1024]{2,1,0:T(8,128)(2,1)}), bf16[32,40,1024]{2,1,0:T(8,128)(2,1)S(1)}, u32[]{:S(2)}, u32[]{:S(2)}) %all-to-all-start) | async-done | bytes 2621472 | tf_op jit(solution)/shard_map/all_to_all | solution.py:176
  393.2 6.2 %convolution_bitcast_fusion = f32[1,1280,1024]{2,1,0:T(8,128)} fusion(bf16[1280,1024]{1,0:T(8,128)(2,1)S(1)} %bitcast.102, bf16[1024,1024]{1,0:T(8,128)(2,1)} %bitcast.37), kind=kOutput, calls=%fused_computation.10 | convolution fusion | flops 2684354560 | bytes 9961472 | tf_op jit(solution)/shard_map/erd,edf->erf/dot_general | solution.py:180
  399.4 5.9 %convolution_convert_fusion = bf16[1280,1024]{1,0:T(8,128)(2,1)} fusion(f32[1,1280,1024]{2,1,0:T(8,128)} %convolution_bitcast_fusion, bf16[1,512,1024]{2,1,0:T(8,128)(2,1)} %all-gather.12.cloned.1.call-done), kind=kOutput, calls=%fused_computation.13 | convolution fusion | flops 1347420160 | bytes 8912896 | tf_op jit(solution)/shard_map/erf,efd->erd/dot_general | solution.py:190
  405.3 4.0 all-to-all-start.2
  409.3 0.1 copy.110
  409.4 122.2 %all-to-all-done.2 = bf16[32,40,1024]{2,1,0:T(8,128)(2,1)S(1)} async-done(((bf16[32,40,1024]{2,1,0:T(8,128)(2,1)}), bf16[32,40,1024]{2,1,0:T(8,128)(2,1)S(1)}, u32[]{:S(2)}, u32[]{:S(2)}) %all-to-all-start.2) | async-done | bytes 2621472 | tf_op jit(solution)/shard_map/all_to_all | solution.py:196
  531.6 5.4 gather_fusion
  537.0 2.9 fusion.6
  539.9 0.8 fusion.26
  (71 shorter events, 1.6 us)
Async XLA Ops:
  7.2 40.0 %copy-start.2 = (bf16[1,128,1024]{2,1,0:T(8,128)(2,1)S(1)}, bf16[1,128,1024]{2,1,0:T(8,128)(2,1)}, u32[]{:S(2)}) copy-start(bf16[1,128,1024]{2,1,0:T(8,128)(2,1)} %param.11) | copy-start | bytes 786436
  7.2 40.1 %copy-start.9 = (f32[1024]{0:T(1024)S(1)}, f32[1024]{0:T(1024)}, u32[]{:S(2)}) copy-start(f32[1024]{0:T(1024)} %param.16) | copy-start | bytes 12292
  7.2 40.2 %copy-start.11 = (s32[1,3]{1,0:T(1,128)S(1)}, s32[1,3]{1,0:T(1,128)}, u32[]{:S(2)}) copy-start(s32[1,3]{1,0:T(1,128)} %param.12) | copy-start | bytes 40
  7.2 98.1 %all-gather.6.cloned.1.call-start = ((), (), s32[]{:S(2)}) async-start(), calls=%async_computation.3 | async-start | bytes 2228224 | tf_op jit(solution)/shard_map/all_gather | solution.py:59
  47.1 135.8 %all-gather.8.cloned.1.call-start = ((), (), s32[]{:S(2)}) async-start(), calls=%async_computation.4 | async-start | bytes 4325376 | tf_op jit(solution)/shard_map/all_gather | solution.py:145
  47.3 62.1 %copy-start.6 = (bf16[1,64,1024]{2,1,0:T(8,128)(2,1)S(1)}, bf16[1,64,1024]{2,1,0:T(8,128)(2,1)}, u32[]{:S(2)}) copy-start(bf16[1,64,1024]{2,1,0:T(8,128)(2,1)} %param.20) | copy-start | bytes 393220
  107.6 0.8 copy-start.4
  111.0 7.3 %copy-start.7 = (s32[1,128,8]{1,2,0:T(8,128)S(1)}, s32[1,128,8]{1,2,0:T(8,128)}, u32[]{:S(2)}) copy-start(s32[1,128,8]{1,2,0:T(8,128)} %param.14) | copy-start | bytes 12292
  111.0 146.7 %all-to-all-start.1 = ((bf16[16,1,64,1024]{3,2,1,0:T(8,128)(2,1)}), bf16[16,1,64,1024]{3,2,1,0:T(8,128)(2,1)}, u32[]{:S(2)}, u32[]{:S(2)}) async-start(bf16[16,1,64,1024]{3,2,1,0:T(8,128)(2,1)} %stack.2), calls=%async_computation.1 | async-start | bytes 4194304 | tf_op jit(solution)/shard_map/all_to_all | solution.py:184
  116.1 125.0 %all-gather.10.cloned.1.call-start = ((), (), s32[]{:S(2)}) async-start(), calls=%async_computation.5 | async-start | bytes 1114112 | tf_op jit(solution)/shard_map/all_gather | solution.py:59
  124.1 12.2 %slice-start = ((f32[128,1024]{1,0:T(8,128)}), f32[128,512]{1,0:T(8,128)S(1)}, s32[]{:S(2)}) async-start(f32[128,1024]{1,0:T(8,128)} %copy-done.4), calls=%async_computation.7 | async-start | bytes 524288 | tf_op jit(solution)/shard_map/slice | solution.py:124
  196.2 6.4 %copy-start = (f32[4,256,4096]{2,1,0:T(8,128)}, f32[4,256,4096]{2,1,0:T(8,128)S(1)}, u32[]{:S(2)}) copy-start(f32[4,256,4096]{2,1,0:T(8,128)S(1)} %get-tuple-element.22) | copy-start | bytes 50331652
  196.2 6.4 %copy-start.1 = (f32[4,256,512]{2,1,0:T(8,128)S(1)}, f32[4,256,512]{2,1,0:T(8,128)}, u32[]{:S(2)}) copy-start(f32[4,256,512]{2,1,0:T(8,128)} %get-tuple-element.20) | copy-start | bytes 6291460
  203.2 11.2 %copy-start.5 = (bf16[512,256]{0,1:T(8,128)(2,1)S(1)}, bf16[512,256]{0,1:T(8,128)(2,1)}, u32[]{:S(2)}) copy-start(bf16[512,256]{0,1:T(8,128)(2,1)} %copy.96) | copy-start | bytes 786436
  214.4 26.7 %copy-start.3 = (bf16[1,128,1024]{2,1,0:T(8,128)(2,1)S(1)}, bf16[1,128,1024]{2,1,0:T(8,128)(2,1)}, u32[]{:S(2)}) copy-start(bf16[1,128,1024]{2,1,0:T(8,128)(2,1)} %param.11) | copy-start | bytes 786436
  214.4 28.4 %copy-start.8 = (f32[1024]{0:T(1024)S(1)}, f32[1024]{0:T(1024)}, u32[]{:S(2)}) copy-start(f32[1024]{0:T(1024)} %param.19) | copy-start | bytes 12292
  257.7 135.5 %all-to-all-start = ((bf16[32,40,1024]{2,1,0:T(8,128)(2,1)}), bf16[32,40,1024]{2,1,0:T(8,128)(2,1)S(1)}, u32[]{:S(2)}, u32[]{:S(2)}) async-start(bf16[32,40,1024]{2,1,0:T(8,128)(2,1)} %bitcast.34), calls=%async_computation | async-start | bytes 5242880 | tf_op jit(solution)/shard_map/all_to_all | solution.py:176
  270.5 128.9 %all-gather.12.cloned.1.call-start = ((), (), s32[]{:S(2)}) async-start(), calls=%async_computation.6 | async-start | bytes 1114112 | tf_op jit(solution)/shard_map/all_gather | solution.py:193
  405.3 4.0 copy-start.10
  405.3 126.3 %all-to-all-start.2 = ((bf16[32,40,1024]{2,1,0:T(8,128)(2,1)}), bf16[32,40,1024]{2,1,0:T(8,128)(2,1)S(1)}, u32[]{:S(2)}, u32[]{:S(2)}) async-start(bf16[32,40,1024]{2,1,0:T(8,128)(2,1)} %bitcast.103), calls=%async_computation.2 | async-start | bytes 5242880 | tf_op jit(solution)/shard_map/all_to_all | solution.py:196
Sparse Core Ops, SparseCore 0:
  47.2 58.0 all-gather.5
  109.5 73.3 all-gather.7
  186.0 55.1 all-gather.9
  274.0 56.7 all-gather.11
